TPU v7x, 1024 devices: a whole 8x8x8 slice. The times are simulated.
1024 devices in a mesh: dp: 32 (over x_lo, y, core), tensor: 32 (over z, x_hi).
Axes of the slice: x: 8 (x_hi: 4, x_lo: 2; x = x_hi * 2 + x_lo), y: 8, z: 8, core: 2. Of those that a mesh axis runs over, the one named last changes fastest.
Arguments:
- x_long: bfloat16 [8192, 64, 128], P('dp', None, 'tensor'), may hold values from -6 to 6
- dv_long: bfloat16 [8192, 1024], P('dp'), may hold values from -0.059814453 to 0.059814453
- x_short: bfloat16 [16384, 64, 128], P('tensor', 'dp'), may hold values from -6 to 6
- dv_short: bfloat16 [16384, 1024], P('tensor'), may hold values from -0.059814453 to 0.059814453
- long_len: int32 [32], P('dp'), may hold values from 64 to 256, as said below
- short_len: int32 [32], P('tensor'), may hold values from 128 to 512, as said below
- master: float32 [64, 128, 1024], P('dp', 'tensor'), may hold values from -0.3 to 0.3
- moment1: float32 [64, 128, 1024], P('dp', 'tensor'), may hold values from -2 to 2
- moment2: float32 [64, 128, 1024], P('dp', 'tensor'), may hold values from 0.1 to 2
Outputs:
- v_long: bfloat16 [8192, 1024], P(('dp', 'tensor'))
- new_master: float32 [64, 128, 1024], P('dp', 'tensor')
- new_moment1: float32 [64, 128, 1024], P('dp', 'tensor')
- new_moment2: float32 [64, 128, 1024], P('dp', 'tensor')
- next_weight: bfloat16 [64, 128, 1024], P(None, 'tensor')
Inputs may be any that keep to these rules, and one draw needn't show every extreme that they name: `long_len`: some group has all 256 rows live; every group has at least 64 and at least one. `short_len`: some group has all 512 rows live; every group has at least 128 and at least one.
All inputs are finite; a program needn't handle non-finite values.
Results may differ from a plain program's by a relative error of at most 0.005.
Values may be sent and summed in bfloat16 or wider, within the bound.
A program may use at most 32 MiB of HBM per device.

v0:
```python
import jax
import jax.numpy as jnp
from jax import lax
from jax.sharding import PartitionSpec as P


def contract_rows(left, right):
    return lax.dot_general(
        left, right, (((0,), (0,)), ((), ())), preferred_element_type=jnp.float32
    )


def body(x_long, dv_long, x_short, dv_short, long_len, short_len, master, moment1, moment2):
    weight_shard = master.astype(jnp.bfloat16)
    long_rows = x_long.shape[0]
    inner_part = x_long.shape[2]
    kv_width = master.shape[2]
    short_rows = x_short.shape[0]
    outer_part = x_short.shape[1]
    inner_whole = x_short.shape[2]
    piece = lax.all_gather(weight_shard, "dp", axis=0, tiled=True)
    inputs = x_long
    flat_inputs = inputs.reshape(long_rows, piece.shape[0] * inner_part)
    flat_piece = piece.reshape(piece.shape[0] * inner_part, kv_width)
    partial_values = jnp.dot(flat_inputs, flat_piece, preferred_element_type=jnp.float32)
    values = lax.psum_scatter(partial_values, "tensor", scatter_dimension=0, tiled=True)
    own_rows = values.shape[0]
    row_start = lax.axis_index("tensor") * own_rows
    own_live = row_start + jnp.arange(own_rows, dtype=jnp.int32) < long_len[0]
    v_long = jnp.where(own_live[:, None], values, jnp.float32(0.0)).astype(jnp.bfloat16)
    long_live = jnp.arange(long_rows, dtype=jnp.int32) < long_len[0]
    short_live = jnp.arange(short_rows, dtype=jnp.int32) < short_len[0]
    live_dv_long = jnp.where(long_live[:, None], dv_long, jnp.zeros_like(dv_long))
    live_dv_short = jnp.where(short_live[:, None], dv_short, jnp.zeros_like(dv_short))
    count = lax.axis_size("dp") * master.shape[0]
    inputs = x_long
    flat_inputs = inputs.reshape(long_rows, count * inner_part)
    grad_long = lax.psum_scatter(
        contract_rows(flat_inputs, live_dv_long).reshape(count, inner_part, kv_width),
        "dp",
        scatter_dimension=0,
        tiled=True,
    )
    inputs = x_short
    flat_inputs = inputs.reshape(short_rows, outer_part * inner_whole)
    product = contract_rows(flat_inputs, live_dv_short).reshape(outer_part, inner_whole, kv_width)
    summed = lax.psum(jnp.swapaxes(product, 0, 1), "tensor")
    owned = lax.dynamic_slice_in_dim(
        summed, lax.axis_index("tensor") * master.shape[1], master.shape[1], 0
    )
    grad_short = jnp.swapaxes(owned, 0, 1)
    grad = grad_long + grad_short
    new_moment1 = 0.9 * moment1 + 0.1 * grad
    new_moment2 = 0.999 * moment2 + 0.001 * grad * grad
    first_corr = 1.0 - 0.9**10
    second_corr = 1.0 - 0.999**10
    update = new_moment1 / first_corr / (jnp.sqrt(new_moment2 / second_corr) + 1e-08)
    new_master = master - 0.01 * (update + 0.1 * master)
    next_weight = lax.all_gather(new_master.astype(jnp.bfloat16), "dp", axis=0, tiled=True)
    return (v_long, new_master, new_moment1, new_moment2, next_weight)


def solution(mesh):
    placed = (
        P("dp", None, "tensor"),
        P("dp", None),
        P("tensor", "dp", None),
        P("tensor", None),
        P("dp"),
        P("tensor"),
        P("dp", "tensor", None),
        P("dp", "tensor", None),
        P("dp", "tensor", None),
    )
    return jax.shard_map(
        body,
        mesh=mesh,
        in_specs=placed,
        out_specs=(
            P(("dp", "tensor"), None),
            P("dp", "tensor", None),
            P("dp", "tensor", None),
            P("dp", "tensor", None),
            P(None, "tensor", None),
        ),
        check_vma=False,
    )
```

profile of v0, /device:TPU:1, one launch (start us, length us, event | category | flops | bytes accessed | tf_op | source)
XLA Modules:
  0.0 859.8 jit_solution(17987521606308425600)
XLA Ops:
  7.2 0.0 all-reduce.6.cloned.1.call-start
  7.9 0.9 reshape.37
  8.8 1.4 convolution_bitcast_fusion
  10.2 0.0 copy-start.5
  10.2 1.3 reshape.38
  11.5 0.0 copy-start.4
  11.5 0.0 all-reduce.6.cloned.1.call-update
  11.6 0.0 all-reduce.4.cloned.1.call-start
  12.3 0.0 copy-done.5
  12.4 0.4 copy-done.4
  12.8 1.5 fusion
  14.3 0.0 copy-start.2
  14.3 0.0 copy-start.3
  14.3 0.0 all-reduce.4.cloned.1.call-update
  14.3 0.0 copy-start.1
  14.3 0.0 reduce-scatter.2.cloned.1.call-start
  14.4 1.3 dynamic-slice
  16.3 244.6 %all-reduce.6.cloned.1.call-done = f32[64,4,1024]{2,1,0:T(4,128)} async-done(((f32[64,4,1024]{2,1,0:T(4,128)}), f32[64,4,1024]{2,1,0:T(4,128)}) %all-reduce.6.cloned.1.call-update) | async-done | bytes 1048592
  260.9 310.2 %all-reduce.4.cloned.1.call-done = f32[128,2,1024]{2,0,1:T(8,128)} async-done(((f32[128,2,1024]{2,0,1:T(8,128)}), f32[128,2,1024]{2,0,1:T(8,128)}) %all-reduce.4.cloned.1.call-update) | async-done | bytes 1048592 | tf_op jit(solution)/shard_map/psum | solution.py:47
  571.1 0.0 copy-done.2
  571.1 0.0 copy-done.3
  571.1 0.0 copy-done.1
  571.1 1.5 fusion.14
  572.6 0.0 copy-start
  572.6 58.3 %all_gather.6 = bf16[64,4,1024]{2,1,0:T(4,128)(2,1)S(1)} all-gather(bf16[2,4,1024]{2,1,0:T(4,128)(2,1)S(1)} %get-tuple-element.9), channel_id=1, replica_groups=mesh['dp'=32,'tensor'=32] {'dp'}, dimensions={0}, use_global_device_ids=true | all-gather | bytes 540672 | tf_op jit(solution)/shard_map/all_gather | solution.py:21
  630.9 0.0 copy-done
  630.9 1.3 convolution_bitcast_fusion.1
  632.2 0.0 reduce-scatter.2.cloned.1.call-update
  632.3 32.1 %all_gather.7 = bf16[64,4,1024]{2,1,0:T(4,128)(2,1)S(1)} all-gather(bf16[2,4,1024]{2,1,0:T(4,128)(2,1)S(1)} %get-tuple-element.5), channel_id=1, replica_groups=mesh['dp'=32,'tensor'=32] {'dp'}, dimensions={0}, use_global_device_ids=true | all-gather | bytes 540672 | tf_op jit(solution)/shard_map/all_gather | solution.py:59
  664.4 186.6 %reduce-scatter.2.cloned.1.call-done = f32[8,1024]{1,0:T(8,128)} async-done(((f32[256,1024]{1,0:T(8,128)}), f32[8,1024]{1,0:T(8,128)}) %reduce-scatter.2.cloned.1.call-update) | async-done | bytes 32784 | tf_op jit(solution)/shard_map/reduce_scatter | solution.py:26
  851.1 1.4 select_convert_fusion
  852.5 0.8 copy.32
  (3 shorter events, 0.0 us)
Async XLA Ops:
  7.2 253.7 %all-reduce.6.cloned.1.call-start = ((), (), s32[]{:S(2)}) async-start(), calls=%async_computation.3 | async-start | bytes 2097152
  10.2 2.1 copy-start.5
  11.5 1.2 copy-start.4
  11.6 559.5 %all-reduce.4.cloned.1.call-start = ((), (), s32[]{:S(2)}) async-start(), calls=%async_computation.2 | async-start | bytes 2097152 | tf_op jit(solution)/shard_map/psum | solution.py:47
  14.3 556.8 %copy-start.2 = (f32[2,4,1024]{2,1,0:T(4,128)S(1)}, f32[2,4,1024]{2,1,0:T(4,128)}, u32[]{:S(2)}) copy-start(f32[2,4,1024]{2,1,0:T(4,128)} %param.16) | copy-start | bytes 98308
  14.3 556.8 %copy-start.3 = (f32[2,4,1024]{2,1,0:T(4,128)S(1)}, f32[2,4,1024]{2,1,0:T(4,128)}, u32[]{:S(2)}) copy-start(f32[2,4,1024]{2,1,0:T(4,128)} %param.17) | copy-start | bytes 98308
  14.3 556.8 %copy-start.1 = (f32[2,4,1024]{2,1,0:T(4,128)S(1)}, f32[2,4,1024]{2,1,0:T(4,128)}, u32[]{:S(2)}) copy-start(f32[2,4,1024]{2,1,0:T(4,128)} %param.15) | copy-start | bytes 98308
  14.3 836.7 %reduce-scatter.2.cloned.1.call-start = ((), (), s32[]{:S(2)}) async-start(), calls=%async_computation.1 | async-start | bytes 1081344 | tf_op jit(solution)/shard_map/reduce_scatter | solution.py:26
  572.6 58.3 %copy-start = (bf16[256,64,4]{0,2,1:T(4,128)(2,1)S(1)}, bf16[256,64,4]{0,2,1:T(4,128)(2,1)}, u32[]{:S(2)}) copy-start(bf16[256,64,4]{0,2,1:T(4,128)(2,1)} %param.9) | copy-start | bytes 393220
Sparse Core Ops, SparseCore 0:
  11.7 249.1 all-reduce.5
  264.4 306.6 all-reduce.3
  632.4 218.6 reduce-scatter.1
where the time goes:
time: 864 us; the launch traced here: 860 us
  waiting for transfers between devices  741 us (86%)
  blocking collectives  90.4 us (10%)
  between operations  15.8 us (2%)
    psum x1, waiting for transfers between devices, body(): summed = lax.psum(jnp.swapaxes(product, 0, 1), 'tensor')  310 us
    unnamed x4, waiting for transfers between devices  245 us
    reduce_scatter x1, waiting for transfers between devices, body(): lax.psum_scatter(partial_values, 'tensor', scatter_dimension=0, tiled=True)  187 us
    all_gather x1, blocking collectives, body(): piece = lax.all_gather(weight_shard, 'dp', axis=0, tiled=True)  58.3 us
    all_gather x1, blocking collectives, body(): lax.all_gather(new_master.astype(jnp.bfloat16), 'dp', axis=0, tiled=True)  32.1 us
  transfers between devices with their start and end apart: 3, of which 3 were waited for; matrix products, arithmetic and copies ran while one was open for 0% of the time, Pallas kernels for 0%

commit v1 on v0

v1 whole, which is shorter than its diff:
```python
import jax
import jax.numpy as jnp
from jax import lax
from jax.experimental import pallas as pl
from jax.experimental.pallas import tpu as pltpu
from jax.sharding import PartitionSpec as P

MESH = pl.DeviceIdType.MESH
F32 = jnp.float32
BF16 = jnp.bfloat16

NZ, NX = 8, 4
NQ, NC = 16, 2


def contract(left, right, left_dim):
    return lax.dot_general(
        left, right, (((left_dim,), (0,)), ((), ())), preferred_element_type=F32
    )


def kernel(
    xt_ref, dvl_ref, xs_ref, dvs_ref, llen_ref, slen_ref, m_ref, m1_ref, m2_ref,
    v_out, nm_out, nm1_out, nm2_out, nw_out,
    gl, gs, vp, wown, wbuf, nown,
    rc, c1, rq, sz, rsz, rsx, vz, rvz, rvx,
    send, recv,
):
    dp = lax.axis_index("dp")
    tensor = lax.axis_index("tensor")
    q, core = dp // NC, dp % NC
    z, xh = tensor // NX, tensor % NX
    kv = v_out.shape[1]

    def at_z(k):
        return (dp, lax.rem(z + k, NZ) * NX + xh)

    def at_x(k):
        return (dp, z * NX + lax.rem(xh + k, NX))

    def at_q(k):
        return (lax.rem(q + k, NQ) * NC + core, tensor)

    other = (q * NC + (1 - core), tensor)

    barrier = pltpu.get_barrier_semaphore()

    def greet(device):
        pl.semaphore_signal(barrier, inc=1, device_id=device, device_id_type=MESH)

    lax.fori_loop(1, NZ, lambda k, c: (greet(at_z(k)), c)[1], 0)
    lax.fori_loop(1, NX, lambda k, c: (greet(at_x(k)), c)[1], 0)
    lax.fori_loop(1, NQ, lambda k, c: (greet(at_q(k)), c)[1], 0)
    greet(other)

    def remote(src, dst, slot, device):
        pltpu.make_async_remote_copy(
            src_ref=src, dst_ref=dst, send_sem=send.at[slot], recv_sem=recv.at[slot],
            device_id=device, device_id_type=MESH,
        ).start()

    def wait(sem, ref):
        pltpu.make_async_copy(ref, ref, sem).wait()

    w = jnp.concatenate([m_ref[0], m_ref[1]], axis=0).astype(BF16)
    wown[...] = w

    rows = lax.broadcasted_iota(jnp.int32, dvs_ref.shape, 0)
    dvs = jnp.where(rows < slen_ref[0], dvs_ref[...], jnp.zeros_like(dvs_ref[...]))
    g = contract(xs_ref[...], dvs, 0)
    half = g.shape[0] // 2
    g0 = g[:half].reshape(half // 8, 8, kv)
    g1 = g[half:].reshape(half // 8, 8, kv)
    low = lax.broadcasted_iota(jnp.int32, g0.shape, 1) < 4
    even = jnp.where(low, g0, pltpu.roll(g1, 4, 1)).astype(BF16)
    odd = jnp.where(low, pltpu.roll(g0, 4, 1), g1).astype(BF16)
    gs[:, 0] = even
    gs[:, 1] = odd

    rows = lax.broadcasted_iota(jnp.int32, dvl_ref.shape, 0)
    dvl = jnp.where(rows < llen_ref[0], dvl_ref[...], jnp.zeros_like(dvl_ref[...]))
    gl[...] = contract(xt_ref[...], dvl, 1).astype(BF16).reshape(gl.shape)

    pl.semaphore_wait(barrier, NZ - 1 + NX - 1 + NQ - 1 + 1)

    def start(k, c):
        to = lax.rem(z + k, NZ)
        remote(gs.at[pl.ds(2 * to, 2)], rsz.at[k - 1], 0, at_z(k))
        return c

    lax.fori_loop(1, NZ, start, 0)

    def start(k, c):
        remote(wown, wbuf.at[q, core], 1, at_q(k))
        return c

    lax.fori_loop(1, NQ, start, 0)
    wbuf[q, core] = w

    remote(gl.at[:, 1 - core], rc, 2, other)
    wait(recv.at[2], rc)

    def add(i, c):
        c1[i] = (gl[i, core].astype(F32) + rc[i].astype(F32)).astype(BF16)
        return c

    lax.fori_loop(0, NQ, add, 0)

    def start(k, c):
        remote(c1.at[lax.rem(q + k, NQ)], rq.at[k - 1], 3, at_q(k))
        return c

    lax.fori_loop(1, NQ, start, 0)

    wait(recv.at[1], rq)
    remote(wbuf.at[:, core], wbuf.at[:, core], 4, other)
    wait(recv.at[4], rc)
    weights = wbuf[...].reshape(NQ * NC * 8, kv)
    vp[...] = contract(xt_ref[...], weights, 0).astype(BF16).reshape(vp.shape)

    def start(k, c):
        to = lax.rem(z + k, NZ)
        remote(vp.at[pl.ds(2 * to, 2)], rvz.at[k - 1], 5, at_z(k))
        return c

    lax.fori_loop(1, NZ, start, 0)

    wait(recv.at[0], rsz)
    total = gs[pl.ds(2 * z, 2)].astype(F32)
    for k in range(NZ - 1):
        total += rsz[k].astype(F32)
    sz[...] = total.astype(BF16).reshape(sz.shape)

    def start(k, c):
        remote(sz.at[lax.rem(xh + k, NX)], rsx.at[k - 1], 6, at_x(k))
        return c

    lax.fori_loop(1, NX, start, 0)

    wait(recv.at[3], rq)
    grad = c1[q].astype(F32)
    for k in range(NQ - 1):
        grad += rq[k].astype(F32)

    wait(recv.at[6], rsx)
    short = sz[xh].astype(F32)
    for k in range(NX - 1):
        short += rsx[k].astype(F32)
    grad += short

    first_corr = 1.0 - 0.9**10
    second_corr = 1.0 - 0.999**10
    for a in range(2):
        ga = grad[4 * a : 4 * a + 4]
        master = m_ref[a]
        new1 = 0.9 * m1_ref[a] + 0.1 * ga
        new2 = 0.999 * m2_ref[a] + 0.001 * ga * ga
        update = new1 / first_corr / (jnp.sqrt(new2 / second_corr) + 1e-08)
        new_master = master - 0.01 * (update + 0.1 * master)
        nm_out[a] = new_master
        nm1_out[a] = new1
        nm2_out[a] = new2
        nown[a] = new_master.astype(BF16)

    def start(k, c):
        remote(nown, nw_out.at[q, core], 7, at_q(k))
        return c

    lax.fori_loop(1, NQ, start, 0)
    nw_out[q, core] = nown[...]

    wait(recv.at[5], rvz)
    total = vp[pl.ds(2 * z, 2)].astype(F32)
    for k in range(NZ - 1):
        total += rvz[k].astype(F32)
    vz[...] = total.astype(BF16).reshape(vz.shape)

    def start(k, c):
        remote(vz.at[lax.rem(xh + k, NX)], rvx.at[k - 1], 8, at_x(k))
        return c

    lax.fori_loop(1, NX, start, 0)

    wait(recv.at[7], nw_out.at[pl.ds(0, NQ - 1), core])
    remote(nw_out.at[:, core], nw_out.at[:, core], 9, other)

    wait(recv.at[8], rvx)
    values = vz[xh].astype(F32)
    for k in range(NX - 1):
        values += rvx[k].astype(F32)
    own_row = tensor * 8 + lax.broadcasted_iota(jnp.int32, values.shape, 0)
    v_out[...] = jnp.where(own_row < llen_ref[0], values, 0.0).astype(BF16)

    wait(recv.at[9], nw_out.at[:, core])

    wait(send.at[0], rsz)
    wait(send.at[1], rq)
    wait(send.at[2], rc)
    wait(send.at[3], rq)
    wait(send.at[4], rc)
    wait(send.at[5], rvz)
    wait(send.at[6], rsx)
    wait(send.at[7], nw_out.at[pl.ds(0, NQ - 1), core])
    wait(send.at[8], rvx)
    wait(send.at[9], nw_out.at[:, core])


def body(x_long, dv_long, x_short, dv_short, long_len, short_len, master, moment1, moment2):
    kv = master.shape[2]
    rows_l = x_long.shape[0]
    xt = jnp.transpose(x_long, (1, 2, 0)).reshape(-1, rows_l)
    xs = x_short.reshape(x_short.shape[0], -1)
    state = jax.ShapeDtypeStruct(master.shape, F32)
    vmem = pl.BlockSpec(memory_space=pltpu.VMEM)
    smem = pl.BlockSpec(memory_space=pltpu.SMEM)
    v, nm, nm1, nm2, nw = pl.pallas_call(
        kernel,
        out_shape=(
            jax.ShapeDtypeStruct((8, kv), BF16),
            state,
            state,
            state,
            jax.ShapeDtypeStruct((NQ, NC, 2, 4, kv), BF16),
        ),
        in_specs=[vmem] * 4 + [smem] * 2 + [vmem] * 3,
        out_specs=(vmem,) * 5,
        scratch_shapes=[
            pltpu.VMEM((NQ, NC, 8, kv), BF16),
            pltpu.VMEM((NZ * NX // 2, 2, 8, kv), BF16),
            pltpu.VMEM((NZ * NX // 2, 2, 8, kv), BF16),
            pltpu.VMEM((8, kv), BF16),
            pltpu.VMEM((NQ, NC, 8, kv), BF16),
            pltpu.VMEM((2, 4, kv), BF16),
            pltpu.VMEM((NQ, 8, kv), BF16),
            pltpu.VMEM((NQ, 8, kv), BF16),
            pltpu.VMEM((NQ - 1, 8, kv), BF16),
            pltpu.VMEM((NX, 8, kv), BF16),
            pltpu.VMEM((NZ - 1, 2, 2, 8, kv), BF16),
            pltpu.VMEM((NX - 1, 8, kv), BF16),
            pltpu.VMEM((NX, 8, kv), BF16),
            pltpu.VMEM((NZ - 1, 2, 2, 8, kv), BF16),
            pltpu.VMEM((NX - 1, 8, kv), BF16),
            pltpu.SemaphoreType.DMA((10,)),
            pltpu.SemaphoreType.DMA((10,)),
        ],
        compiler_params=pltpu.CompilerParams(collective_id=0, has_side_effects=True),
    )(xt, dv_long, xs, dv_short, long_len, short_len, master, moment1, moment2)
    return v, nm, nm1, nm2, nw.reshape(NQ * NC * 2, 4, kv)


def solution(mesh):
    placed = (
        P("dp", None, "tensor"),
        P("dp", None),
        P("tensor", "dp", None),
        P("tensor", None),
        P("dp"),
        P("tensor"),
        P("dp", "tensor", None),
        P("dp", "tensor", None),
        P("dp", "tensor", None),
    )
    return jax.shard_map(
        body,
        mesh=mesh,
        in_specs=placed,
        out_specs=(
            P(("dp", "tensor"), None),
            P("dp", "tensor", None),
            P("dp", "tensor", None),
            P("dp", "tensor", None),
            P(None, "tensor", None),
        ),
        check_vma=False,
    )
```

time: 864 us -> 67.6 us (0.08)
  waiting for transfers between devices: 741 us -> 0 us
  blocking collectives: 90.4 us -> 0 us
  Pallas kernels: 0 us -> 57.3 us
  between operations: 15.8 us -> 2 us
    psum x1 -> x0, waiting for transfers between devices: 310 us -> none  [body(): summed = lax.psum(jnp.swapaxes(product, 0, 1), 'tensor')]
    unnamed x4 -> x0, waiting for transfers between devices: 245 us -> none
    reduce_scatter x1 -> x0, waiting for transfers between devices: 187 us -> none  [body(): lax.psum_scatter(partial_values, 'tensor', scatter_dimension=0, tiled=True)]
    all_gather x2 -> x0, blocking collectives: 90.4 us -> none  [the longest x1 58.3 us: body(): piece = lax.all_gather(weight_shard, 'dp', axis=0, tiled=True)]
    pallas_call x0 -> x1, Pallas kernels: none -> 57.3 us  [body(): pl.pallas_call(kernel, out_shape=(jax.ShapeDtypeStruct((8, kv), BF16), st...]
  transfers between devices with their start and end apart: 3 -> 0, of which waited for: 3 -> 0; matrix products, arithmetic and copies ran while one was open for 0% -> 0% of each run, Pallas kernels for 0% -> 0%
where the time goes in v1:
time: 67.6 us; the launch traced here: 67.2 us
  Pallas kernels  57.3 us (85%)
  local copies, waits for them, and re-layouts  7.83 us (12%)
  between operations  2 us (3%)
    pallas_call x1, Pallas kernels, body(): pl.pallas_call(kernel, out_shape=(jax.ShapeDtypeStruct((8, kv), BF16), st...  57.3 us
    unnamed x14, local copies, waits for them, and re-layouts  6.24 us
    reshape x1, local copies, waits for them, and re-layouts, body(): xt = jnp.transpose(x_long, (1, 2, 0)).reshape(-1, rows_l)  1.59 us

profile of v1, /device:TPU:1, one launch (start us, length us, event | category | flops | bytes accessed | tf_op | source)
XLA Modules:
  0.0 67.2 jit_solution(17948042974984430234)
XLA Ops:
  0.6 0.0 copy-start
  2.0 1.6 %reshape.19.xt_ref = bf16[256,256]{1,0:T(8,128)(2,1)} reshape(bf16[64,4,256]{2,1,0:T(4,128)(2,1)} %bitcast.9) | data formatting | bytes 262144 | tf_op jit(solution)/shard_map/reshape | solution.py:211
  3.6 0.0 copy-done
  3.6 0.7 %copy.16 = bf16[64,8,2,128]{3,1,2,0:T(8,128)(2,1)} copy(bf16[64,8,2,128]{3,2,1,0:T(2,128)(2,1)S(1)} %bitcast.8) | data formatting | bytes 524288
  4.3 57.3 %shard_map.128 = (bf16[8,1024]{1,0:T(8,128)(2,1)}, f32[2,4,1024]{2,1,0:T(4,128)}, f32[2,4,1024]{2,1,0:T(4,128)}, f32[2,4,1024]{2,1,0:T(4,128)}, bf16[16,2,2,4,1024]{4,3,2,1,0:T(4,128)(2,1)}) custom-call(bf16[256,256]{1,0:T(8,128)(2,1)} %reshape.19.xt_ref, bf16[256,1024]{1,0:T(8,128)(2,1)} %dvl_ref.1, bf16[512,256]{1,0:T(8,128)(2,1)} %bitcast.6, ...), custom_call_target="tpu_custom_call" | custom-call | tf_op jit(solution)/shard_map/pallas_call | solution.py:216
  61.7 0.0 copy-start.3
  61.7 1.3 %copy.24 = bf16[8,1024]{1,0:T(8,128)(2,1)} copy(bf16[8,1024]{1,0:T(8,128)(2,1)} %get-tuple-element.20) | data formatting | bytes 32768
  63.0 0.0 copy-done.3
  63.0 0.0 copy-start.2
  63.0 0.6 copy.25
  63.6 0.2 copy-done.2
  63.8 0.0 copy-start.1
  63.8 0.6 copy.26
  64.4 0.2 copy-done.1
  64.5 0.6 copy.27
  65.2 2.0 %copy.28 = bf16[64,4,1024]{2,1,0:T(4,128)(2,1)} copy(bf16[64,4,1024]{2,1,0:T(4,128)(2,1)} %bitcast.7) | data formatting | bytes 1048576
Async XLA Ops:
  0.6 2.9 %copy-start = (bf16[512,2,128]{2,1,0:T(2,128)(2,1)S(1)}, bf16[512,2,128]{2,1,0:T(2,128)(2,1)}, u32[]{:S(2)}) copy-start(bf16[512,2,128]{2,1,0:T(2,128)(2,1)} %param.11) | copy-start | bytes 786436
  61.7 1.3 %copy-start.3 = (f32[2,4,1024]{2,1,0:T(4,128)S(1)}, f32[2,4,1024]{2,1,0:T(4,128)}, u32[]{:S(2)}) copy-start(f32[2,4,1024]{2,1,0:T(4,128)} %get-tuple-element.21) | copy-start | bytes 98308
  63.0 0.8 %copy-start.2 = (f32[2,4,1024]{2,1,0:T(4,128)S(1)}, f32[2,4,1024]{2,1,0:T(4,128)}, u32[]{:S(2)}) copy-start(f32[2,4,1024]{2,1,0:T(4,128)} %get-tuple-element.22) | copy-start | bytes 98308
  63.8 0.8 %copy-start.1 = (f32[2,4,1024]{2,1,0:T(4,128)S(1)}, f32[2,4,1024]{2,1,0:T(4,128)}, u32[]{:S(2)}) copy-start(f32[2,4,1024]{2,1,0:T(4,128)} %get-tuple-element.23) | copy-start | bytes 98308

commit v2 on v0

v2 whole, which is shorter than its diff:
```python
import jax
import jax.numpy as jnp
from jax import lax
from jax.experimental import pallas as pl
from jax.experimental.pallas import tpu as pltpu
from jax.sharding import PartitionSpec as P

MESH = pl.DeviceIdType.MESH
F32 = jnp.float32
BF16 = jnp.bfloat16

NZ, NX = 8, 4
NY, NC = 8, 2
NQ = 2 * NY
W, WF, GC, GQ, N, NF, S1, V1 = 0, 1, 2, 3, 4, 5, 6, 10


def contract(left, right, left_dim):
    return lax.dot_general(
        left, right, (((left_dim,), (0,)), ((), ())), preferred_element_type=F32
    )


def far_first(i):
    return lax.rem(4 + ((i + 1) // 2) * (2 * lax.rem(i, 2) - 1) + 8, 8)


def loop(n, f):
    def step(i, c):
        f(i)
        return c

    lax.fori_loop(0, n, step, 0)


def swap_quads(even, odd):
    low = lax.broadcasted_iota(jnp.int32, even.shape, 1) < 4
    return (
        jnp.where(low, even, pltpu.roll(odd, 4, 1)),
        jnp.where(low, pltpu.roll(even, 4, 1), odd),
    )


def kernel(
    xl_hbm, dvl_hbm, xs_hbm, dvs_hbm, llen_ref, slen_ref, m_hbm, m1_hbm, m2_hbm,
    v_out, nm_out, nm1_out, nm2_out, nw_out,
    xl_ref, dvl_ref, xs_ref, dvs_ref, m_ref, m1_ref, m2_ref,
    xsf, xt, gl, gs, vp, wown, wbuf, nown,
    rc, c1, rq,
    s_rz, s_rx, s_sz, s_sx, s_rzx, s_rxz,
    v_rz, v_rx, v_sz, v_sx, v_rzx, v_rxz,
    load, send, recv, recv_w, recv_n,
):
    dp = lax.axis_index("dp")
    tensor = lax.axis_index("tensor")
    q, core = dp // NC, lax.rem(dp, NC)
    z, xh = tensor // NX, lax.rem(tensor, NX)
    xl, y = q // NY, lax.rem(q, NY)
    kv = v_out.shape[1]
    cols = kv // 2

    def to_z(k):
        return lax.rem(z + k, NZ)

    def to_x(k):
        return lax.rem(xh + k, NX)

    def at_z(k):
        return (dp, to_z(k) * NX + xh)

    def at_x(k):
        return (dp, z * NX + to_x(k))

    def at_q(p):
        return (p * NC + core, tensor)

    def step_q(i):
        far = far_first(i // 2)
        side = lax.rem(xl + 1 - lax.rem(i, 2), 2) * NY
        return side + lax.rem(y + far, NY), side + lax.rem(y - far + NY, NY)

    other = (q * NC + (1 - core), tensor)
    barrier = pltpu.get_barrier_semaphore()

    def greet(device):
        pl.semaphore_signal(barrier, inc=1, device_id=device, device_id_type=MESH)

    loop(NQ - 1, lambda i: greet(at_q(step_q(i)[0])))
    loop(NZ - 1, lambda i: greet(at_z(far_first(i))))
    loop(NX - 1, lambda i: greet(at_x(i + 1)))
    greet(other)

    loads = [
        pltpu.make_async_copy(src, dst, load.at[i])
        for i, (src, dst) in enumerate((
            (m_hbm, m_ref), (xs_hbm, xs_ref), (dvs_hbm, dvs_ref),
            (xl_hbm, xl_ref), (dvl_hbm, dvl_ref), (m1_hbm, m1_ref), (m2_hbm, m2_ref),
        ))
    ]
    for copy in loads:
        copy.start()

    def remote(src, dst, slot, device, arrival=None):
        pltpu.make_async_remote_copy(
            src_ref=src, dst_ref=dst, send_sem=send.at[slot],
            recv_sem=recv.at[slot] if arrival is None else arrival,
            device_id=device, device_id_type=MESH,
        ).start()

    def wait(sem, ref):
        pltpu.make_async_copy(ref, ref, sem).wait()

    def to_other_chips(own, gathered, slot, arrivals):
        remote(own, gathered.at[q, core], slot + 1, other)
        loop(
            NQ - 1,
            lambda i: remote(
                own, gathered.at[q, core], slot, at_q(step_q(i)[0]), arrivals.at[i]
            ),
        )

    def on_to_other_core(gathered, slot, arrivals):
        def forward(i):
            chunk = gathered.at[step_q(i)[1], core]
            wait(arrivals.at[i], chunk)
            remote(chunk, chunk, slot + 1, other)

        loop(NQ - 1, forward)
        wait(recv.at[slot + 1], gathered.at[:, 1 - core])

    def first_stage(part, rz, rx, slot):
        def along_z(i):
            k = far_first(i)
            remote(part.at[0, to_z(k)], rz.at[k - 1], slot, at_z(k))

        loop(NZ - 1, along_z)
        for k in (2, 1, 3):
            remote(part.at[1, :, to_x(k)], rx.at[k - 1], slot + 1, at_x(k))

    def second_stage(part, rz, rx, sz, sx, rzx, rxz, slot):
        wait(recv.at[slot], rz)
        total = part[0, z].astype(F32)
        for k in range(NZ - 1):
            total += rz[k].astype(F32)
        sz[...] = total.astype(BF16)
        for k in (2, 1, 3):
            remote(sz.at[to_x(k)], rzx.at[k - 1], slot + 2, at_x(k))

        wait(recv.at[slot + 1], rx)
        total = part[1, :, xh].astype(F32)
        for k in range(NX - 1):
            total += rx[k].astype(F32)
        sx[...] = total.astype(BF16)

        def along_z(i):
            k = far_first(i)
            remote(sx.at[to_z(k)], rxz.at[k - 1], slot + 3, at_z(k))

        loop(NZ - 1, along_z)

    def last_sums(sz, sx, rzx, rxz, slot):
        wait(recv.at[slot + 2], rzx)
        left = sz[xh].astype(F32)
        for k in range(NX - 1):
            left += rzx[k].astype(F32)
        wait(recv.at[slot + 3], rxz)
        right = sx[z].astype(F32)
        for k in range(NZ - 1):
            right += rxz[k].astype(F32)
        return jnp.concatenate([left, right], axis=1)

    loads[0].wait()
    w = jnp.concatenate([m_ref[0], m_ref[1]], axis=0).astype(BF16)
    wown[...] = w
    pl.semaphore_wait(barrier, NZ - 1 + NX - 1 + NQ - 1 + 1)
    to_other_chips(wown, wbuf, W, recv_w)
    wbuf[q, core] = w

    loads[1].wait()
    xsf[...] = xs_ref[...].astype(F32)
    rows = xs_ref.shape[0] // 2
    live = lax.broadcasted_iota(jnp.int32, (rows, xs_ref.shape[1]), 0) < slen_ref[0]
    x0 = jnp.where(live, xsf[pl.ds(0, rows, stride=2), :], 0.0).astype(BF16)
    x1 = jnp.where(live, xsf[pl.ds(1, rows, stride=2), :], 0.0).astype(BF16)
    loads[2].wait()
    dvs = dvs_ref[...]
    g0 = contract(x0, dvs, 0).reshape(16, 8, kv)
    g1 = contract(x1, dvs, 0).reshape(16, 8, kv)
    for s, owners in enumerate(swap_quads(g0, g1)):
        owners = owners.astype(BF16).reshape(NZ, 2, 8, kv)
        for h in range(2):
            for p in range(2):
                gs[h, :, 2 * p + s] = owners[:, p, :, h * cols : (h + 1) * cols]
    first_stage(gs, s_rz, s_rx, S1)

    loads[3].wait()
    quads = xl_ref[...].astype(F32).reshape(32, 2, 8, 128)
    blocks = swap_quads(quads[:, 0], quads[:, 1])
    x = jnp.concatenate([b.reshape(256, 128) for b in blocks], axis=1)
    live = lax.broadcasted_iota(jnp.int32, x.shape, 1) < llen_ref[0]
    x = jnp.where(live, x, 0.0).astype(BF16)
    xt[...] = x
    loads[4].wait()
    gl[...] = contract(x, dvl_ref[...], 1).astype(BF16).reshape(gl.shape)
    remote(gl.at[:, 1 - core], rc, GC, other)
    wait(recv.at[GC], rc)

    def add(i):
        c1[i] = (gl[i, core].astype(F32) + rc[i].astype(F32)).astype(BF16)

    loop(NQ, add)

    def to_owner(i):
        to = step_q(i)[0]
        remote(c1.at[to], rq.at[i], GQ, at_q(to))

    loop(NQ - 1, to_owner)

    on_to_other_core(wbuf, W, recv_w)
    values = contract(xt[...], wbuf[...].reshape(NQ * NC * 8, kv), 0).astype(BF16)
    for h in range(2):
        part = values[:, h * cols : (h + 1) * cols]
        vp[h] = part.reshape(NZ, NX, 8, cols)
    first_stage(vp, v_rz, v_rx, V1)

    second_stage(gs, s_rz, s_rx, s_sz, s_sx, s_rzx, s_rxz, S1)
    wait(recv.at[GQ], rq)
    grad = c1[q].astype(F32)
    for k in range(NQ - 1):
        grad += rq[k].astype(F32)
    grad += last_sums(s_sz, s_sx, s_rzx, s_rxz, S1)

    loads[5].wait()
    loads[6].wait()
    first_corr = 1.0 - 0.9**10
    second_corr = 1.0 - 0.999**10
    for a in range(2):
        ga = grad[4 * a : 4 * a + 4]
        master = m_ref[a]
        new1 = 0.9 * m1_ref[a] + 0.1 * ga
        new2 = 0.999 * m2_ref[a] + 0.001 * ga * ga
        update = new1 / first_corr / (jnp.sqrt(new2 / second_corr) + 1e-08)
        new_master = master - 0.01 * (update + 0.1 * master)
        nown[a] = new_master.astype(BF16)
        nm_out[a] = new_master
        nm1_out[a] = new1
        nm2_out[a] = new2
    to_other_chips(nown, nw_out, N, recv_n)
    nw_out[q, core] = nown[...]

    second_stage(vp, v_rz, v_rx, v_sz, v_sx, v_rzx, v_rxz, V1)
    on_to_other_core(nw_out, N, recv_n)
    v_out[...] = last_sums(v_sz, v_sx, v_rzx, v_rxz, V1).astype(BF16)

    wait(send.at[W], rq)
    wait(send.at[WF], rc)
    wait(send.at[GC], rc)
    wait(send.at[GQ], rq)
    wait(send.at[N], rq)
    wait(send.at[NF], rc)
    for slot, (rz, rx, rzx, rxz) in (
        (S1, (s_rz, s_rx, s_rzx, s_rxz)),
        (V1, (v_rz, v_rx, v_rzx, v_rxz)),
    ):
        wait(send.at[slot], rz)
        wait(send.at[slot + 1], rx)
        wait(send.at[slot + 2], rzx)
        wait(send.at[slot + 3], rxz)


def hand_over(*refs):
    n = len(refs) // 2
    copies = [
        pltpu.make_async_copy(refs[i], refs[n + i], refs[-1].at[i]) for i in range(n)
    ]
    for copy in copies:
        copy.start()
    for copy in copies:
        copy.wait()


def body(x_long, dv_long, x_short, dv_short, long_len, short_len, master, moment1, moment2):
    kv = master.shape[2]
    cols = kv // 2
    rows_l, outer, inner = x_long.shape
    xl = jnp.transpose(x_long, (1, 2, 0)).reshape(outer, inner, rows_l // 128, 128)
    xl = jnp.transpose(xl, (0, 2, 1, 3)).reshape(-1, 128)
    xs = x_short.reshape(-1, x_short.shape[2])
    operands = (xl, dv_long, xs, dv_short, long_len, short_len, master, moment1, moment2)
    state = jax.ShapeDtypeStruct(master.shape, F32)
    outs = (
        jax.ShapeDtypeStruct((8, kv), BF16),
        state,
        state,
        state,
        jax.ShapeDtypeStruct((NQ, NC, 2, 4, kv), BF16),
    )
    vmem = pl.BlockSpec(memory_space=pltpu.VMEM)
    hbm = pl.BlockSpec(memory_space=pl.ANY)
    smem = pl.BlockSpec(memory_space=pltpu.SMEM)
    sums = [
        pltpu.VMEM((NZ - 1, NX, 8, cols), BF16),
        pltpu.VMEM((NX - 1, NZ, 8, cols), BF16),
        pltpu.VMEM((NX, 8, cols), BF16),
        pltpu.VMEM((NZ, 8, cols), BF16),
        pltpu.VMEM((NX - 1, 8, cols), BF16),
        pltpu.VMEM((NZ - 1, 8, cols), BF16),
    ]
    results = pl.pallas_call(
        kernel,
        out_shape=tuple(pltpu.VMEM(o.shape, o.dtype) for o in outs),
        in_specs=[hbm] * 4 + [smem] * 2 + [hbm] * 3,
        out_specs=(vmem,) * 5,
        scratch_shapes=[
            pltpu.VMEM(a.shape, a.dtype) for a in operands if a.dtype != jnp.int32
        ]
        + [
            pltpu.VMEM(xs.shape, F32),
            pltpu.VMEM((outer * inner, rows_l), BF16),
            pltpu.VMEM((NQ, NC, 8, kv), BF16),
            pltpu.VMEM((2, NZ, NX, 8, cols), BF16),
            pltpu.VMEM((2, NZ, NX, 8, cols), BF16),
            pltpu.VMEM((8, kv), BF16),
            pltpu.VMEM((NQ, NC, 8, kv), BF16),
            pltpu.VMEM((2, 4, kv), BF16),
            pltpu.VMEM((NQ, 8, kv), BF16),
            pltpu.VMEM((NQ, 8, kv), BF16),
            pltpu.VMEM((NQ - 1, 8, kv), BF16),
        ]
        + sums
        + sums
        + [
            pltpu.SemaphoreType.DMA((7,)),
            pltpu.SemaphoreType.DMA((14,)),
            pltpu.SemaphoreType.DMA((14,)),
            pltpu.SemaphoreType.DMA((NQ - 1,)),
            pltpu.SemaphoreType.DMA((NQ - 1,)),
        ],
        compiler_params=pltpu.CompilerParams(collective_id=0, has_side_effects=True),
    )(*operands)
    v, nm, nm1, nm2, nw = pl.pallas_call(
        hand_over,
        out_shape=outs,
        in_specs=[vmem] * 5,
        out_specs=(hbm,) * 5,
        scratch_shapes=[pltpu.SemaphoreType.DMA((5,))],
    )(*(pltpu.with_memory_space_constraint(r, pltpu.VMEM) for r in results))
    return v, nm, nm1, nm2, nw.reshape(NQ * NC * 2, 4, kv)


def solution(mesh):
    placed = (
        P("dp", None, "tensor"),
        P("dp", None),
        P("tensor", "dp", None),
        P("tensor", None),
        P("dp"),
        P("tensor"),
        P("dp", "tensor", None),
        P("dp", "tensor", None),
        P("dp", "tensor", None),
    )
    return jax.shard_map(
        body,
        mesh=mesh,
        in_specs=placed,
        out_specs=(
            P(("dp", "tensor"), None),
            P("dp", "tensor", None),
            P("dp", "tensor", None),
            P("dp", "tensor", None),
            P(None, "tensor", None),
        ),
        check_vma=False,
    )
```

time: 864 us -> 56.3 us (0.07)
  waiting for transfers between devices: 741 us -> 0 us
  blocking collectives: 90.4 us -> 0 us
  Pallas kernels: 0 us -> 54.2 us
  between operations: 15.8 us -> 1.93 us
    psum x1 -> x0, waiting for transfers between devices: 310 us -> none  [body(): summed = lax.psum(jnp.swapaxes(product, 0, 1), 'tensor')]
    unnamed x4 -> x0, waiting for transfers between devices: 245 us -> none
    reduce_scatter x1 -> x0, waiting for transfers between devices: 187 us -> none  [body(): lax.psum_scatter(partial_values, 'tensor', scatter_dimension=0, tiled=True)]
    all_gather x2 -> x0, blocking collectives: 90.4 us -> none  [the longest x1 58.3 us: body(): piece = lax.all_gather(weight_shard, 'dp', axis=0, tiled=True)]
    pallas_call x0 -> x2, Pallas kernels: none -> 54.2 us  [the longest x1 53.4 us: body(): pl.pallas_call(kernel, out_shape=tuple((pltpu.VMEM(o.shape, o.dtype) for...]
  transfers between devices with their start and end apart: 3 -> 0, of which waited for: 3 -> 0; matrix products, arithmetic and copies ran while one was open for 0% -> 0% of each run, Pallas kernels for 0% -> 0%
where the time goes in v2:
time: 56.3 us; the launch traced here: 56.2 us
  Pallas kernels  54.2 us (96%)
  between operations  1.93 us (3%)
    pallas_call x1, Pallas kernels, body(): pl.pallas_call(kernel, out_shape=tuple((pltpu.VMEM(o.shape, o.dtype) for...  53.4 us

profile of v2, /device:TPU:1, one launch (start us, length us, event | category | flops | bytes accessed | tf_op | source)
XLA Modules:
  0.0 56.2 jit_solution(17267228237523069682)
XLA Ops:
  1.9 53.4 %shard_map.128 = (bf16[8,1024]{1,0:T(8,128)(2,1)S(1)}, f32[2,4,1024]{2,1,0:T(4,128)S(1)}, f32[2,4,1024]{2,1,0:T(4,128)S(1)}, f32[2,4,1024]{2,1,0:T(4,128)S(1)}, bf16[16,2,2,4,1024]{4,3,2,1,0:T(4,128)(2,1)S(1)}) custom-call(bf16[512,128]{1,0:T(8,128)(2,1)} %bitcast.10, bf16[256,1024]{1,0:T(8,128)(2,1)} %dvl_hbm.1, bf16[1024,128]{1,0:T(8,128)(2,1)} %bitcast.9, ...), custom_call_target="tpu_custom_call" | custom-call | tf_op jit(solution)/shard_map/pallas_call | solution.py:309
  55.3 0.9 %shard_map.129 = (bf16[8,1024]{1,0:T(8,128)(2,1)}, f32[2,4,1024]{2,1,0:T(4,128)}, f32[2,4,1024]{2,1,0:T(4,128)}, f32[2,4,1024]{2,1,0:T(4,128)}, bf16[16,2,2,4,1024]{4,3,2,1,0:T(4,128)(2,1)}) custom-call(bf16[8,1024]{1,0:T(8,128)(2,1)S(1)} %get-tuple-element.15.refs_0_, f32[2,4,1024]{2,1,0:T(4,128)S(1)} %get-tuple-element.16.refs_1_, ...), custom_call_target="tpu_custom_call" | custom-call | tf_op jit(solution)/shard_map/pallas_call | solution.py:341

commit v3 on v2

--- a/solution.py
+++ b/solution.py
@@ -93,8 +93,9 @@
     loads = [
         pltpu.make_async_copy(src, dst, load.at[i])
         for i, (src, dst) in enumerate((
-            (m_hbm, m_ref), (xs_hbm, xs_ref), (dvs_hbm, dvs_ref),
-            (xl_hbm, xl_ref), (dvl_hbm, dvl_ref), (m1_hbm, m1_ref), (m2_hbm, m2_ref),
+            (xs_hbm, xs_ref), (dvs_hbm, dvs_ref), (m_hbm, m_ref),
+            (xl_hbm, xl_ref), (dvl_hbm, dvl_ref),
+            (m1_hbm, m1_ref), (m2_hbm, m2_ref),
         ))
     ]
     for copy in loads:
@@ -126,7 +127,6 @@
             remote(chunk, chunk, slot + 1, other)
 
         loop(NQ - 1, forward)
-        wait(recv.at[slot + 1], gathered.at[:, 1 - core])
 
     def first_stage(part, rz, rx, slot):
         def along_z(i):
@@ -170,19 +170,12 @@
         return jnp.concatenate([left, right], axis=1)
 
     loads[0].wait()
-    w = jnp.concatenate([m_ref[0], m_ref[1]], axis=0).astype(BF16)
-    wown[...] = w
-    pl.semaphore_wait(barrier, NZ - 1 + NX - 1 + NQ - 1 + 1)
-    to_other_chips(wown, wbuf, W, recv_w)
-    wbuf[q, core] = w
-
-    loads[1].wait()
     xsf[...] = xs_ref[...].astype(F32)
     rows = xs_ref.shape[0] // 2
     live = lax.broadcasted_iota(jnp.int32, (rows, xs_ref.shape[1]), 0) < slen_ref[0]
     x0 = jnp.where(live, xsf[pl.ds(0, rows, stride=2), :], 0.0).astype(BF16)
     x1 = jnp.where(live, xsf[pl.ds(1, rows, stride=2), :], 0.0).astype(BF16)
-    loads[2].wait()
+    loads[1].wait()
     dvs = dvs_ref[...]
     g0 = contract(x0, dvs, 0).reshape(16, 8, kv)
     g1 = contract(x1, dvs, 0).reshape(16, 8, kv)
@@ -191,7 +184,11 @@
         for h in range(2):
             for p in range(2):
                 gs[h, :, 2 * p + s] = owners[:, p, :, h * cols : (h + 1) * cols]
-    first_stage(gs, s_rz, s_rx, S1)
+
+    loads[2].wait()
+    w = jnp.concatenate([m_ref[0], m_ref[1]], axis=0).astype(BF16)
+    wown[...] = w
+    wbuf[q, core] = w
 
     loads[3].wait()
     quads = xl_ref[...].astype(F32).reshape(32, 2, 8, 128)
@@ -202,7 +199,12 @@
     xt[...] = x
     loads[4].wait()
     gl[...] = contract(x, dvl_ref[...], 1).astype(BF16).reshape(gl.shape)
+
+    pl.semaphore_wait(barrier, NZ - 1 + NX - 1 + NQ - 1 + 1)
     remote(gl.at[:, 1 - core], rc, GC, other)
+    to_other_chips(wown, wbuf, W, recv_w)
+    first_stage(gs, s_rz, s_rx, S1)
+
     wait(recv.at[GC], rc)
 
     def add(i):
@@ -217,13 +219,15 @@
     loop(NQ - 1, to_owner)
 
     on_to_other_core(wbuf, W, recv_w)
+    second_stage(gs, s_rz, s_rx, s_sz, s_sx, s_rzx, s_rxz, S1)
+
+    wait(recv.at[WF], wbuf.at[:, 1 - core])
     values = contract(xt[...], wbuf[...].reshape(NQ * NC * 8, kv), 0).astype(BF16)
     for h in range(2):
         part = values[:, h * cols : (h + 1) * cols]
         vp[h] = part.reshape(NZ, NX, 8, cols)
     first_stage(vp, v_rz, v_rx, V1)
 
-    second_stage(gs, s_rz, s_rx, s_sz, s_sx, s_rzx, s_rxz, S1)
     wait(recv.at[GQ], rq)
     grad = c1[q].astype(F32)
     for k in range(NQ - 1):
@@ -251,6 +255,7 @@
     second_stage(vp, v_rz, v_rx, v_sz, v_sx, v_rzx, v_rxz, V1)
     on_to_other_core(nw_out, N, recv_n)
     v_out[...] = last_sums(v_sz, v_sx, v_rzx, v_rxz, V1).astype(BF16)
+    wait(recv.at[NF], nw_out.at[:, 1 - core])
 
     wait(send.at[W], rq)
     wait(send.at[WF], rc)

time: 56.3 us -> 51.8 us (0.920)
  Pallas kernels: 54.2 us -> 49.7 us
    pallas_call x1, Pallas kernels: 53.4 us -> 48.8 us  [body(): pl.pallas_call(kernel, out_shape=tuple((pltpu.VMEM(o.shape, o.dtype) for...]
where the time goes in v3:
time: 51.8 us; the launch traced here: 51.6 us
  Pallas kernels  49.7 us (96%)
  between operations  1.93 us (4%)
    pallas_call x1, Pallas kernels, body(): pl.pallas_call(kernel, out_shape=tuple((pltpu.VMEM(o.shape, o.dtype) for...  48.8 us

profile of v3, /device:TPU:1, one launch (start us, length us, event | category | flops | bytes accessed | tf_op | source)
XLA Modules:
  0.0 51.6 jit_solution(3438001083171275529)
XLA Ops:
  1.9 48.8 %shard_map.128 = (bf16[8,1024]{1,0:T(8,128)(2,1)S(1)}, f32[2,4,1024]{2,1,0:T(4,128)S(1)}, f32[2,4,1024]{2,1,0:T(4,128)S(1)}, f32[2,4,1024]{2,1,0:T(4,128)S(1)}, bf16[16,2,2,4,1024]{4,3,2,1,0:T(4,128)(2,1)S(1)}) custom-call(bf16[512,128]{1,0:T(8,128)(2,1)} %bitcast.10, bf16[256,1024]{1,0:T(8,128)(2,1)} %dvl_hbm.1, bf16[1024,128]{1,0:T(8,128)(2,1)} %bitcast.9, ...), custom_call_target="tpu_custom_call" | custom-call | tf_op jit(solution)/shard_map/pallas_call | solution.py:314
  50.7 0.9 %shard_map.129 = (bf16[8,1024]{1,0:T(8,128)(2,1)}, f32[2,4,1024]{2,1,0:T(4,128)}, f32[2,4,1024]{2,1,0:T(4,128)}, f32[2,4,1024]{2,1,0:T(4,128)}, bf16[16,2,2,4,1024]{4,3,2,1,0:T(4,128)(2,1)}) custom-call(bf16[8,1024]{1,0:T(8,128)(2,1)S(1)} %get-tuple-element.15.refs_0_, f32[2,4,1024]{2,1,0:T(4,128)S(1)} %get-tuple-element.16.refs_1_, ...), custom_call_target="tpu_custom_call" | custom-call | tf_op jit(solution)/shard_map/pallas_call | solution.py:346

commit v4 on v3

--- a/solution.py
+++ b/solution.py
@@ -45,7 +45,7 @@
     xl_hbm, dvl_hbm, xs_hbm, dvs_hbm, llen_ref, slen_ref, m_hbm, m1_hbm, m2_hbm,
     v_out, nm_out, nm1_out, nm2_out, nw_out,
     xl_ref, dvl_ref, xs_ref, dvs_ref, m_ref, m1_ref, m2_ref,
-    xsf, xt, gl, gs, vp, wown, wbuf, nown,
+    xsf, xt, gl, gsz, gsx, vpz, vpx, wown, wbuf, nown,
     rc, c1, rq,
     s_rz, s_rx, s_sz, s_sx, s_rzx, s_rxz,
     v_rz, v_rx, v_sz, v_sx, v_rzx, v_rxz,
@@ -57,7 +57,7 @@
     z, xh = tensor // NX, lax.rem(tensor, NX)
     xl, y = q // NY, lax.rem(q, NY)
     kv = v_out.shape[1]
-    cols = kv // 2
+    cols = v_sz.shape[2]
 
     def to_z(k):
         return lax.rem(z + k, NZ)
@@ -120,26 +120,29 @@
             ),
         )
 
-    def on_to_other_core(gathered, slot, arrivals):
+    def on_to_other_core(gathered, slot, arrivals, between=None):
         def forward(i):
             chunk = gathered.at[step_q(i)[1], core]
             wait(arrivals.at[i], chunk)
             remote(chunk, chunk, slot + 1, other)
 
-        loop(NQ - 1, forward)
-
-    def first_stage(part, rz, rx, slot):
+        loop(8, forward)
+        if between is not None:
+            loop(NQ - 1, between)
+        loop(NQ - 9, lambda i: forward(i + 8))
+
+    def first_stage(part_z, part_x, rz, rx, slot):
         def along_z(i):
             k = far_first(i)
-            remote(part.at[0, to_z(k)], rz.at[k - 1], slot, at_z(k))
+            remote(part_z.at[to_z(k)], rz.at[k - 1], slot, at_z(k))
 
         loop(NZ - 1, along_z)
         for k in (2, 1, 3):
-            remote(part.at[1, :, to_x(k)], rx.at[k - 1], slot + 1, at_x(k))
-
-    def second_stage(part, rz, rx, sz, sx, rzx, rxz, slot):
+            remote(part_x.at[:, to_x(k)], rx.at[k - 1], slot + 1, at_x(k))
+
+    def second_stage(part_z, part_x, rz, rx, sz, sx, rzx, rxz, slot):
         wait(recv.at[slot], rz)
-        total = part[0, z].astype(F32)
+        total = part_z[z].astype(F32)
         for k in range(NZ - 1):
             total += rz[k].astype(F32)
         sz[...] = total.astype(BF16)
@@ -147,7 +150,7 @@
             remote(sz.at[to_x(k)], rzx.at[k - 1], slot + 2, at_x(k))
 
         wait(recv.at[slot + 1], rx)
-        total = part[1, :, xh].astype(F32)
+        total = part_x[:, xh].astype(F32)
         for k in range(NX - 1):
             total += rx[k].astype(F32)
         sx[...] = total.astype(BF16)
@@ -181,9 +184,9 @@
     g1 = contract(x1, dvs, 0).reshape(16, 8, kv)
     for s, owners in enumerate(swap_quads(g0, g1)):
         owners = owners.astype(BF16).reshape(NZ, 2, 8, kv)
-        for h in range(2):
-            for p in range(2):
-                gs[h, :, 2 * p + s] = owners[:, p, :, h * cols : (h + 1) * cols]
+        for p in range(2):
+            gsz[:, 2 * p + s] = owners[:, p, :, :cols]
+            gsx[:, 2 * p + s] = owners[:, p, :, cols:]
 
     loads[2].wait()
     w = jnp.concatenate([m_ref[0], m_ref[1]], axis=0).astype(BF16)
@@ -203,7 +206,7 @@
     pl.semaphore_wait(barrier, NZ - 1 + NX - 1 + NQ - 1 + 1)
     remote(gl.at[:, 1 - core], rc, GC, other)
     to_other_chips(wown, wbuf, W, recv_w)
-    first_stage(gs, s_rz, s_rx, S1)
+    first_stage(gsz, gsx, s_rz, s_rx, S1)
 
     wait(recv.at[GC], rc)
 
@@ -216,17 +219,15 @@
         to = step_q(i)[0]
         remote(c1.at[to], rq.at[i], GQ, at_q(to))
 
-    loop(NQ - 1, to_owner)
-
-    on_to_other_core(wbuf, W, recv_w)
-    second_stage(gs, s_rz, s_rx, s_sz, s_sx, s_rzx, s_rxz, S1)
+
+    on_to_other_core(wbuf, W, recv_w, to_owner)
+    second_stage(gsz, gsx, s_rz, s_rx, s_sz, s_sx, s_rzx, s_rxz, S1)
 
     wait(recv.at[WF], wbuf.at[:, 1 - core])
     values = contract(xt[...], wbuf[...].reshape(NQ * NC * 8, kv), 0).astype(BF16)
-    for h in range(2):
-        part = values[:, h * cols : (h + 1) * cols]
-        vp[h] = part.reshape(NZ, NX, 8, cols)
-    first_stage(vp, v_rz, v_rx, V1)
+    vpz[...] = values[:, :cols].reshape(vpz.shape)
+    vpx[...] = values[:, cols:].reshape(vpx.shape)
+    first_stage(vpz, vpx, v_rz, v_rx, V1)
 
     wait(recv.at[GQ], rq)
     grad = c1[q].astype(F32)
@@ -252,7 +253,7 @@
     to_other_chips(nown, nw_out, N, recv_n)
     nw_out[q, core] = nown[...]
 
-    second_stage(vp, v_rz, v_rx, v_sz, v_sx, v_rzx, v_rxz, V1)
+    second_stage(vpz, vpx, v_rz, v_rx, v_sz, v_sx, v_rzx, v_rxz, V1)
     on_to_other_core(nw_out, N, recv_n)
     v_out[...] = last_sums(v_sz, v_sx, v_rzx, v_rxz, V1).astype(BF16)
     wait(recv.at[NF], nw_out.at[:, 1 - core])
@@ -286,7 +287,8 @@
 
 def body(x_long, dv_long, x_short, dv_short, long_len, short_len, master, moment1, moment2):
     kv = master.shape[2]
-    cols = kv // 2
+    cols = 5 * kv // 8
+    rest = kv - cols
     rows_l, outer, inner = x_long.shape
     xl = jnp.transpose(x_long, (1, 2, 0)).reshape(outer, inner, rows_l // 128, 128)
     xl = jnp.transpose(xl, (0, 2, 1, 3)).reshape(-1, 128)
@@ -305,11 +307,11 @@
     smem = pl.BlockSpec(memory_space=pltpu.SMEM)
     sums = [
         pltpu.VMEM((NZ - 1, NX, 8, cols), BF16),
-        pltpu.VMEM((NX - 1, NZ, 8, cols), BF16),
+        pltpu.VMEM((NX - 1, NZ, 8, rest), BF16),
         pltpu.VMEM((NX, 8, cols), BF16),
-        pltpu.VMEM((NZ, 8, cols), BF16),
+        pltpu.VMEM((NZ, 8, rest), BF16),
         pltpu.VMEM((NX - 1, 8, cols), BF16),
-        pltpu.VMEM((NZ - 1, 8, cols), BF16),
+        pltpu.VMEM((NZ - 1, 8, rest), BF16),
     ]
     results = pl.pallas_call(
         kernel,
@@ -323,8 +325,10 @@
             pltpu.VMEM(xs.shape, F32),
             pltpu.VMEM((outer * inner, rows_l), BF16),
             pltpu.VMEM((NQ, NC, 8, kv), BF16),
-            pltpu.VMEM((2, NZ, NX, 8, cols), BF16),
-            pltpu.VMEM((2, NZ, NX, 8, cols), BF16),
+            pltpu.VMEM((NZ, NX, 8, cols), BF16),
+            pltpu.VMEM((NZ, NX, 8, rest), BF16),
+            pltpu.VMEM((NZ, NX, 8, cols), BF16),
+            pltpu.VMEM((NZ, NX, 8, rest), BF16),
             pltpu.VMEM((8, kv), BF16),
             pltpu.VMEM((NQ, NC, 8, kv), BF16),
             pltpu.VMEM((2, 4, kv), BF16),

time: 51.8 us -> 50.8 us (0.981)
  Pallas kernels: 49.7 us -> 48.7 us
    pallas_call x1, Pallas kernels: 48.8 us -> 47.8 us  [body(): pl.pallas_call(kernel, out_shape=tuple((pltpu.VMEM(o.shape, o.dtype) for...]
where the time goes in v4:
time: 50.8 us; the launch traced here: 50.6 us
  Pallas kernels  48.7 us (96%)
  between operations  1.93 us (4%)
    pallas_call x1, Pallas kernels, body(): pl.pallas_call(kernel, out_shape=tuple((pltpu.VMEM(o.shape, o.dtype) for...  47.8 us

profile of v4, /device:TPU:1, one launch (start us, length us, event | category | flops | bytes accessed | tf_op | source)
XLA Modules:
  0.0 50.6 jit_solution(17982042024472016575)
XLA Ops:
  1.9 47.8 %shard_map.128 = (bf16[8,1024]{1,0:T(8,128)(2,1)S(1)}, f32[2,4,1024]{2,1,0:T(4,128)S(1)}, f32[2,4,1024]{2,1,0:T(4,128)S(1)}, f32[2,4,1024]{2,1,0:T(4,128)S(1)}, bf16[16,2,2,4,1024]{4,3,2,1,0:T(4,128)(2,1)S(1)}) custom-call(bf16[512,128]{1,0:T(8,128)(2,1)} %bitcast.10, bf16[256,1024]{1,0:T(8,128)(2,1)} %dvl_hbm.1, bf16[1024,128]{1,0:T(8,128)(2,1)} %bitcast.9, ...), custom_call_target="tpu_custom_call" | custom-call | tf_op jit(solution)/shard_map/pallas_call | solution.py:316
  49.7 0.9 %shard_map.129 = (bf16[8,1024]{1,0:T(8,128)(2,1)}, f32[2,4,1024]{2,1,0:T(4,128)}, f32[2,4,1024]{2,1,0:T(4,128)}, f32[2,4,1024]{2,1,0:T(4,128)}, bf16[16,2,2,4,1024]{4,3,2,1,0:T(4,128)(2,1)}) custom-call(bf16[8,1024]{1,0:T(8,128)(2,1)S(1)} %get-tuple-element.15.refs_0_, f32[2,4,1024]{2,1,0:T(4,128)S(1)} %get-tuple-element.16.refs_1_, ...), custom_call_target="tpu_custom_call" | custom-call | tf_op jit(solution)/shard_map/pallas_call | solution.py:350

commit v5 on v4

--- a/solution.py
+++ b/solution.py
@@ -22,15 +22,12 @@
 
 
 def far_first(i):
-    return lax.rem(4 + ((i + 1) // 2) * (2 * lax.rem(i, 2) - 1) + 8, 8)
+    return (4 + (i + 1) // 2 * (2 * (i % 2) - 1)) % 8
 
 
 def loop(n, f):
-    def step(i, c):
+    for i in range(n):
         f(i)
-        return c
-
-    lax.fori_loop(0, n, step, 0)
 
 
 def swap_quads(even, odd):
@@ -76,7 +73,7 @@
 
     def step_q(i):
         far = far_first(i // 2)
-        side = lax.rem(xl + 1 - lax.rem(i, 2), 2) * NY
+        side = (xl if i % 2 else 1 - xl) * NY
         return side + lax.rem(y + far, NY), side + lax.rem(y - far + NY, NY)
 
     other = (q * NC + (1 - core), tensor)
@@ -210,10 +207,11 @@
 
     wait(recv.at[GC], rc)
 
-    def add(i):
+    def add(i, c):
         c1[i] = (gl[i, core].astype(F32) + rc[i].astype(F32)).astype(BF16)
-
-    loop(NQ, add)
+        return c
+
+    lax.fori_loop(0, NQ, add, 0)
 
     def to_owner(i):
         to = step_q(i)[0]

time: 50.8 us -> 50.8 us (level)
  no operation moved by 1% of the time
where the time goes in v5:
time: 50.8 us; the launch traced here: 50.6 us
  Pallas kernels  48.7 us (96%)
  between operations  1.93 us (4%)
    pallas_call x1, Pallas kernels, body(): pl.pallas_call(kernel, out_shape=tuple((pltpu.VMEM(o.shape, o.dtype) for...  47.8 us

profile of v5, /device:TPU:1, one launch (start us, length us, event | category | flops | bytes accessed | tf_op | source)
XLA Modules:
  0.0 50.6 jit_solution(6336970203939329152)
XLA Ops:
  1.9 47.8 %shard_map.128 = (bf16[8,1024]{1,0:T(8,128)(2,1)S(1)}, f32[2,4,1024]{2,1,0:T(4,128)S(1)}, f32[2,4,1024]{2,1,0:T(4,128)S(1)}, f32[2,4,1024]{2,1,0:T(4,128)S(1)}, bf16[16,2,2,4,1024]{4,3,2,1,0:T(4,128)(2,1)S(1)}) custom-call(bf16[512,128]{1,0:T(8,128)(2,1)} %bitcast.10, bf16[256,1024]{1,0:T(8,128)(2,1)} %dvl_hbm.1, bf16[1024,128]{1,0:T(8,128)(2,1)} %bitcast.9, ...), custom_call_target="tpu_custom_call" | custom-call | tf_op jit(solution)/shard_map/pallas_call | solution.py:314
  49.7 0.9 %shard_map.129 = (bf16[8,1024]{1,0:T(8,128)(2,1)}, f32[2,4,1024]{2,1,0:T(4,128)}, f32[2,4,1024]{2,1,0:T(4,128)}, f32[2,4,1024]{2,1,0:T(4,128)}, bf16[16,2,2,4,1024]{4,3,2,1,0:T(4,128)(2,1)}) custom-call(bf16[8,1024]{1,0:T(8,128)(2,1)S(1)} %get-tuple-element.15.refs_0_, f32[2,4,1024]{2,1,0:T(4,128)S(1)} %get-tuple-element.16.refs_1_, ...), custom_call_target="tpu_custom_call" | custom-call | tf_op jit(solution)/shard_map/pallas_call | solution.py:348

commit v6 on v5

--- a/solution.py
+++ b/solution.py
@@ -12,7 +12,7 @@
 NZ, NX = 8, 4
 NY, NC = 8, 2
 NQ = 2 * NY
-W, WF, GC, GQ, N, NF, S1, V1 = 0, 1, 2, 3, 4, 5, 6, 10
+W, WF, N, NF, GC, GQ, S1, V1 = 0, 2, 4, 6, 8, 9, 10, 14
 
 
 def contract(left, right, left_dim):
@@ -108,66 +108,78 @@
     def wait(sem, ref):
         pltpu.make_async_copy(ref, ref, sem).wait()
 
-    def to_other_chips(own, gathered, slot, arrivals):
-        remote(own, gathered.at[q, core], slot + 1, other)
+    parts = (slice(0, cols), slice(cols, kv))
+
+    def to_other_chips(p, own, gathered, slot, arrivals):
+        mine = own.at[..., parts[p]]
+        there = gathered.at[q, core].at[..., parts[p]]
+        remote(mine, there, slot + 2 + p, other)
         loop(
             NQ - 1,
             lambda i: remote(
-                own, gathered.at[q, core], slot, at_q(step_q(i)[0]), arrivals.at[i]
+                mine, there, slot + p, at_q(step_q(i)[0]), arrivals.at[p, i // 2]
             ),
         )
 
-    def on_to_other_core(gathered, slot, arrivals, between=None):
-        def forward(i):
-            chunk = gathered.at[step_q(i)[1], core]
-            wait(arrivals.at[i], chunk)
-            remote(chunk, chunk, slot + 1, other)
-
-        loop(8, forward)
-        if between is not None:
-            loop(NQ - 1, between)
-        loop(NQ - 9, lambda i: forward(i + 8))
-
-    def first_stage(part_z, part_x, rz, rx, slot):
-        def along_z(i):
+    def on_to_other_core(p, gathered, slot, arrivals):
+        for pair in range(NY):
+            steps = range(2 * pair, min(2 * pair + 2, NQ - 1))
+            arrived = gathered.at[pl.ds(0, len(steps)), core]
+            wait(arrivals.at[p, pair], arrived.at[..., parts[p]])
+            for i in steps:
+                chunk = gathered.at[step_q(i)[1], core].at[..., parts[p]]
+                remote(chunk, chunk, slot + 2 + p, other)
+
+    def of_other_core(p, gathered, slot):
+        wait(recv.at[slot + 2 + p], gathered.at[:, 1 - core].at[..., parts[p]])
+
+    def all_sent(gathered, slot):
+        for p in range(2):
+            sent = gathered.at[pl.ds(0, NQ - 1), core]
+            wait(send.at[slot + p], sent.at[..., parts[p]])
+            wait(send.at[slot + 2 + p], gathered.at[:, core].at[..., parts[p]])
+
+    def first_z(part, rz, slot):
+        for i in range(NZ - 1):
             k = far_first(i)
-            remote(part_z.at[to_z(k)], rz.at[k - 1], slot, at_z(k))
-
-        loop(NZ - 1, along_z)
+            remote(part.at[to_z(k)], rz.at[k - 1], slot, at_z(k))
+
+    def first_x(part, rx, slot):
         for k in (2, 1, 3):
-            remote(part_x.at[:, to_x(k)], rx.at[k - 1], slot + 1, at_x(k))
-
-    def second_stage(part_z, part_x, rz, rx, sz, sx, rzx, rxz, slot):
+            remote(part.at[:, to_x(k)], rx.at[k - 1], slot + 1, at_x(k))
+
+    def second_z(part, rz, sz, rzx, slot):
         wait(recv.at[slot], rz)
-        total = part_z[z].astype(F32)
+        total = part[z].astype(F32)
         for k in range(NZ - 1):
             total += rz[k].astype(F32)
         sz[...] = total.astype(BF16)
         for k in (2, 1, 3):
             remote(sz.at[to_x(k)], rzx.at[k - 1], slot + 2, at_x(k))
 
+    def second_x(part, rx, sx, rxz, slot):
         wait(recv.at[slot + 1], rx)
-        total = part_x[:, xh].astype(F32)
+        total = part[:, xh].astype(F32)
         for k in range(NX - 1):
             total += rx[k].astype(F32)
         sx[...] = total.astype(BF16)
-
-        def along_z(i):
+        for i in range(NZ - 1):
             k = far_first(i)
             remote(sx.at[to_z(k)], rxz.at[k - 1], slot + 3, at_z(k))
 
-        loop(NZ - 1, along_z)
-
-    def last_sums(sz, sx, rzx, rxz, slot):
+    def last_z(sz, rzx, slot):
         wait(recv.at[slot + 2], rzx)
-        left = sz[xh].astype(F32)
+        total = sz[xh].astype(F32)
         for k in range(NX - 1):
-            left += rzx[k].astype(F32)
+            total += rzx[k].astype(F32)
+        return total
+
+    def last_x(sx, rxz, slot):
         wait(recv.at[slot + 3], rxz)
-        right = sx[z].astype(F32)
+        total = sx[z].astype(F32)
         for k in range(NZ - 1):
-            right += rxz[k].astype(F32)
-        return jnp.concatenate([left, right], axis=1)
+            total += rxz[k].astype(F32)
+        return total
 
     loads[0].wait()
     xsf[...] = xs_ref[...].astype(F32)
@@ -202,8 +214,10 @@
 
     pl.semaphore_wait(barrier, NZ - 1 + NX - 1 + NQ - 1 + 1)
     remote(gl.at[:, 1 - core], rc, GC, other)
-    to_other_chips(wown, wbuf, W, recv_w)
-    first_stage(gsz, gsx, s_rz, s_rx, S1)
+    to_other_chips(0, wown, wbuf, W, recv_w)
+    first_z(gsz, s_rz, S1)
+    first_x(gsx, s_rx, S1)
+    to_other_chips(1, wown, wbuf, W, recv_w)
 
     wait(recv.at[GC], rc)
 
@@ -213,55 +227,65 @@
 
     lax.fori_loop(0, NQ, add, 0)
 
-    def to_owner(i):
+    on_to_other_core(0, wbuf, W, recv_w)
+    for i in range(NQ - 1):
         to = step_q(i)[0]
         remote(c1.at[to], rq.at[i], GQ, at_q(to))
 
-
-    on_to_other_core(wbuf, W, recv_w, to_owner)
-    second_stage(gsz, gsx, s_rz, s_rx, s_sz, s_sx, s_rzx, s_rxz, S1)
-
-    wait(recv.at[WF], wbuf.at[:, 1 - core])
-    values = contract(xt[...], wbuf[...].reshape(NQ * NC * 8, kv), 0).astype(BF16)
-    vpz[...] = values[:, :cols].reshape(vpz.shape)
-    vpx[...] = values[:, cols:].reshape(vpx.shape)
-    first_stage(vpz, vpx, v_rz, v_rx, V1)
-
-    wait(recv.at[GQ], rq)
-    grad = c1[q].astype(F32)
-    for k in range(NQ - 1):
-        grad += rq[k].astype(F32)
-    grad += last_sums(s_sz, s_sx, s_rzx, s_rxz, S1)
+    second_x(gsx, s_rx, s_sx, s_rxz, S1)
+    of_other_core(0, wbuf, W)
+    weights = wbuf[:, :, :, :cols].reshape(NQ * NC * 8, cols)
+    vpz[...] = contract(xt[...], weights, 0).astype(BF16).reshape(vpz.shape)
+    first_z(vpz, v_rz, V1)
+
+    on_to_other_core(1, wbuf, W, recv_w)
+    second_z(gsz, s_rz, s_sz, s_rzx, S1)
+    of_other_core(1, wbuf, W)
+    weights = wbuf[:, :, :, cols:].reshape(NQ * NC * 8, kv - cols)
+    vpx[...] = contract(xt[...], weights, 0).astype(BF16).reshape(vpx.shape)
+    first_x(vpx, v_rx, V1)
 
     loads[5].wait()
     loads[6].wait()
+    wait(recv.at[GQ], rq)
     first_corr = 1.0 - 0.9**10
     second_corr = 1.0 - 0.999**10
-    for a in range(2):
-        ga = grad[4 * a : 4 * a + 4]
-        master = m_ref[a]
-        new1 = 0.9 * m1_ref[a] + 0.1 * ga
-        new2 = 0.999 * m2_ref[a] + 0.001 * ga * ga
-        update = new1 / first_corr / (jnp.sqrt(new2 / second_corr) + 1e-08)
-        new_master = master - 0.01 * (update + 0.1 * master)
-        nown[a] = new_master.astype(BF16)
-        nm_out[a] = new_master
-        nm1_out[a] = new1
-        nm2_out[a] = new2
-    to_other_chips(nown, nw_out, N, recv_n)
-    nw_out[q, core] = nown[...]
-
-    second_stage(vpz, vpx, v_rz, v_rx, v_sz, v_sx, v_rzx, v_rxz, V1)
-    on_to_other_core(nw_out, N, recv_n)
-    v_out[...] = last_sums(v_sz, v_sx, v_rzx, v_rxz, V1).astype(BF16)
-    wait(recv.at[NF], nw_out.at[:, 1 - core])
-
-    wait(send.at[W], rq)
-    wait(send.at[WF], rc)
+
+    def update(p, short):
+        part = parts[p]
+        grad = short + c1[q, :, part].astype(F32)
+        for k in range(NQ - 1):
+            grad += rq[k, :, part].astype(F32)
+        for a in range(2):
+            ga = grad[4 * a : 4 * a + 4]
+            master = m_ref[a, :, part]
+            new1 = 0.9 * m1_ref[a, :, part] + 0.1 * ga
+            new2 = 0.999 * m2_ref[a, :, part] + 0.001 * ga * ga
+            step = new1 / first_corr / (jnp.sqrt(new2 / second_corr) + 1e-08)
+            new_master = master - 0.01 * (step + 0.1 * master)
+            nown[a, :, part] = new_master.astype(BF16)
+            nm_out[a, :, part] = new_master
+            nm1_out[a, :, part] = new1
+            nm2_out[a, :, part] = new2
+            nw_out[q, core, a, :, part] = new_master.astype(BF16)
+        to_other_chips(p, nown, nw_out, N, recv_n)
+
+    update(1, last_x(s_sx, s_rxz, S1))
+    update(0, last_z(s_sz, s_rzx, S1))
+
+    second_x(vpx, v_rx, v_sx, v_rxz, V1)
+    second_z(vpz, v_rz, v_sz, v_rzx, V1)
+    on_to_other_core(1, nw_out, N, recv_n)
+    on_to_other_core(0, nw_out, N, recv_n)
+    v_out[:, cols:] = last_x(v_sx, v_rxz, V1).astype(BF16)
+    v_out[:, :cols] = last_z(v_sz, v_rzx, V1).astype(BF16)
+    of_other_core(1, nw_out, N)
+    of_other_core(0, nw_out, N)
+
+    all_sent(wbuf, W)
+    all_sent(nw_out, N)
     wait(send.at[GC], rc)
     wait(send.at[GQ], rq)
-    wait(send.at[N], rq)
-    wait(send.at[NF], rc)
     for slot, (rz, rx, rzx, rxz) in (
         (S1, (s_rz, s_rx, s_rzx, s_rxz)),
         (V1, (v_rz, v_rx, v_rzx, v_rxz)),
@@ -338,10 +362,10 @@
         + sums
         + [
             pltpu.SemaphoreType.DMA((7,)),
-            pltpu.SemaphoreType.DMA((14,)),
-            pltpu.SemaphoreType.DMA((14,)),
-            pltpu.SemaphoreType.DMA((NQ - 1,)),
-            pltpu.SemaphoreType.DMA((NQ - 1,)),
+            pltpu.SemaphoreType.DMA((18,)),
+            pltpu.SemaphoreType.DMA((18,)),
+            pltpu.SemaphoreType.DMA((2, NY)),
+            pltpu.SemaphoreType.DMA((2, NY)),
         ],
         compiler_params=pltpu.CompilerParams(collective_id=0, has_side_effects=True),
     )(*operands)

time: 50.8 us -> 50.4 us (level)
  no operation moved by 1% of the time
where the time goes in v6:
time: 50.4 us; the launch traced here: 50.2 us
  Pallas kernels  48.3 us (96%)
  between operations  1.93 us (4%)
    pallas_call x1, Pallas kernels, body(): pl.pallas_call(kernel, out_shape=tuple((pltpu.VMEM(o.shape, o.dtype) for...  47.4 us

profile of v6, /device:TPU:1, one launch (start us, length us, event | category | flops | bytes accessed | tf_op | source)
XLA Modules:
  0.0 50.2 jit_solution(1141366679735979026)
XLA Ops:
  1.9 47.4 %shard_map.128 = (bf16[8,1024]{1,0:T(8,128)(2,1)S(1)}, f32[2,4,1024]{2,1,0:T(4,128)S(1)}, f32[2,4,1024]{2,1,0:T(4,128)S(1)}, f32[2,4,1024]{2,1,0:T(4,128)S(1)}, bf16[16,2,2,4,1024]{4,3,2,1,0:T(4,128)(2,1)S(1)}) custom-call(bf16[512,128]{1,0:T(8,128)(2,1)} %bitcast.10, bf16[256,1024]{1,0:T(8,128)(2,1)} %dvl_hbm.1, bf16[1024,128]{1,0:T(8,128)(2,1)} %bitcast.9, ...), custom_call_target="tpu_custom_call" | custom-call | tf_op jit(solution)/shard_map/pallas_call | solution.py:338
  49.4 0.9 %shard_map.129 = (bf16[8,1024]{1,0:T(8,128)(2,1)}, f32[2,4,1024]{2,1,0:T(4,128)}, f32[2,4,1024]{2,1,0:T(4,128)}, f32[2,4,1024]{2,1,0:T(4,128)}, bf16[16,2,2,4,1024]{4,3,2,1,0:T(4,128)(2,1)}) custom-call(bf16[8,1024]{1,0:T(8,128)(2,1)S(1)} %get-tuple-element.15.refs_0_, f32[2,4,1024]{2,1,0:T(4,128)S(1)} %get-tuple-element.16.refs_1_, ...), custom_call_target="tpu_custom_call" | custom-call | tf_op jit(solution)/shard_map/pallas_call | solution.py:372

commit v7 on v6

--- a/solution.py
+++ b/solution.py
@@ -227,10 +227,11 @@
 
     lax.fori_loop(0, NQ, add, 0)
 
-    on_to_other_core(0, wbuf, W, recv_w)
     for i in range(NQ - 1):
         to = step_q(i)[0]
         remote(c1.at[to], rq.at[i], GQ, at_q(to))
+
+    on_to_other_core(0, wbuf, W, recv_w)
 
     second_x(gsx, s_rx, s_sx, s_rxz, S1)
     of_other_core(0, wbuf, W)
@@ -238,8 +239,8 @@
     vpz[...] = contract(xt[...], weights, 0).astype(BF16).reshape(vpz.shape)
     first_z(vpz, v_rz, V1)
 
+    second_z(gsz, s_rz, s_sz, s_rzx, S1)
     on_to_other_core(1, wbuf, W, recv_w)
-    second_z(gsz, s_rz, s_sz, s_rzx, S1)
     of_other_core(1, wbuf, W)
     weights = wbuf[:, :, :, cols:].reshape(NQ * NC * 8, kv - cols)
     vpx[...] = contract(xt[...], weights, 0).astype(BF16).reshape(vpx.shape)

time: 50.4 us -> 50.4 us (level)
  no operation moved by 1% of the time
where the time goes in v7:
time: 50.4 us; the launch traced here: 50.2 us
  Pallas kernels  48.3 us (96%)
  between operations  1.93 us (4%)
    pallas_call x1, Pallas kernels, body(): pl.pallas_call(kernel, out_shape=tuple((pltpu.VMEM(o.shape, o.dtype) for...  47.4 us

profile of v7, /device:TPU:1, one launch (start us, length us, event | category | flops | bytes accessed | tf_op | source)
XLA Modules:
  0.0 50.2 jit_solution(18163357858495202119)
XLA Ops:
  1.9 47.4 %shard_map.128 = (bf16[8,1024]{1,0:T(8,128)(2,1)S(1)}, f32[2,4,1024]{2,1,0:T(4,128)S(1)}, f32[2,4,1024]{2,1,0:T(4,128)S(1)}, f32[2,4,1024]{2,1,0:T(4,128)S(1)}, bf16[16,2,2,4,1024]{4,3,2,1,0:T(4,128)(2,1)S(1)}) custom-call(bf16[512,128]{1,0:T(8,128)(2,1)} %bitcast.10, bf16[256,1024]{1,0:T(8,128)(2,1)} %dvl_hbm.1, bf16[1024,128]{1,0:T(8,128)(2,1)} %bitcast.9, ...), custom_call_target="tpu_custom_call" | custom-call | tf_op jit(solution)/shard_map/pallas_call | solution.py:339
  49.3 0.9 %shard_map.129 = (bf16[8,1024]{1,0:T(8,128)(2,1)}, f32[2,4,1024]{2,1,0:T(4,128)}, f32[2,4,1024]{2,1,0:T(4,128)}, f32[2,4,1024]{2,1,0:T(4,128)}, bf16[16,2,2,4,1024]{4,3,2,1,0:T(4,128)(2,1)}) custom-call(bf16[8,1024]{1,0:T(8,128)(2,1)S(1)} %get-tuple-element.15.refs_0_, f32[2,4,1024]{2,1,0:T(4,128)S(1)} %get-tuple-element.16.refs_1_, ...), custom_call_target="tpu_custom_call" | custom-call | tf_op jit(solution)/shard_map/pallas_call | solution.py:373

commit v8 on v7

--- a/solution.py
+++ b/solution.py
@@ -227,11 +227,10 @@
 
     lax.fori_loop(0, NQ, add, 0)
 
+    on_to_other_core(0, wbuf, W, recv_w)
     for i in range(NQ - 1):
         to = step_q(i)[0]
         remote(c1.at[to], rq.at[i], GQ, at_q(to))
-
-    on_to_other_core(0, wbuf, W, recv_w)
 
     second_x(gsx, s_rx, s_sx, s_rxz, S1)
     of_other_core(0, wbuf, W)

time: 50.4 us -> 50.2 us (level)
  no operation moved by 1% of the time
where the time goes in v8:
time: 50.2 us; the launch traced here: 50 us
  Pallas kernels  48.1 us (96%)
  between operations  1.93 us (4%)
    pallas_call x1, Pallas kernels, body(): pl.pallas_call(kernel, out_shape=tuple((pltpu.VMEM(o.shape, o.dtype) for...  47.2 us

profile of v8, /device:TPU:1, one launch (start us, length us, event | category | flops | bytes accessed | tf_op | source)
XLA Modules:
  0.0 50.0 jit_solution(13862840048609040516)
XLA Ops:
  1.9 47.2 %shard_map.128 = (bf16[8,1024]{1,0:T(8,128)(2,1)S(1)}, f32[2,4,1024]{2,1,0:T(4,128)S(1)}, f32[2,4,1024]{2,1,0:T(4,128)S(1)}, f32[2,4,1024]{2,1,0:T(4,128)S(1)}, bf16[16,2,2,4,1024]{4,3,2,1,0:T(4,128)(2,1)S(1)}) custom-call(bf16[512,128]{1,0:T(8,128)(2,1)} %bitcast.10, bf16[256,1024]{1,0:T(8,128)(2,1)} %dvl_hbm.1, bf16[1024,128]{1,0:T(8,128)(2,1)} %bitcast.9, ...), custom_call_target="tpu_custom_call" | custom-call | tf_op jit(solution)/shard_map/pallas_call | solution.py:338
  49.1 0.9 %shard_map.129 = (bf16[8,1024]{1,0:T(8,128)(2,1)}, f32[2,4,1024]{2,1,0:T(4,128)}, f32[2,4,1024]{2,1,0:T(4,128)}, f32[2,4,1024]{2,1,0:T(4,128)}, bf16[16,2,2,4,1024]{4,3,2,1,0:T(4,128)(2,1)}) custom-call(bf16[8,1024]{1,0:T(8,128)(2,1)S(1)} %get-tuple-element.15.refs_0_, f32[2,4,1024]{2,1,0:T(4,128)S(1)} %get-tuple-element.16.refs_1_, ...), custom_call_target="tpu_custom_call" | custom-call | tf_op jit(solution)/shard_map/pallas_call | solution.py:372
